TPU v7x, 32 devices: a whole 2x2x4 slice. The times are simulated.
32 devices in a mesh: fsdp: 8 (over z, x), tp: 4 (over y, core).
Axes of the slice: x: 2, y: 2, z: 4, core: 2. Of those that a mesh axis runs over, the one named last changes fastest.
Arguments:
- inputs: bfloat16 [32768, 512], P(('fsdp', 'tp')), may hold values from -6 to 6
- segments: int32 [8, 4096], P('fsdp', 'tp'), may hold values from 0 to 20, as said below
- out_grad: bfloat16 [32768, 512], P(('fsdp', 'tp')), may hold values from -6 to 6
- first_gain: bfloat16 [512], replicated, may hold values from 0.5 to 1.5
- first_shift: bfloat16 [512], replicated, may hold values from -3 to 3
- qkv_weight: bfloat16 [512, 3, 512], P('fsdp', None, 'tp'), may hold values from -0.375 to 0.375
- qv_bias: bfloat16 [2, 512], replicated, may hold values from -3 to 3
- out_weight: bfloat16 [512, 512], P('tp', 'fsdp'), may hold values from -1 to 1
- out_bias: bfloat16 [512], replicated, may hold values from -3 to 3
- second_gain: bfloat16 [512], replicated, may hold values from 0.5 to 1.5
- second_shift: bfloat16 [512], replicated, may hold values from -3 to 3
- fc_weight: bfloat16 [512, 2048], P('fsdp', 'tp'), may hold values from -0.25 to 0.25
- fc_bias: bfloat16 [2048], replicated, may hold values from -3 to 3
- proj_weight: bfloat16 [2048, 512], P('tp', 'fsdp'), may hold values from -0.125 to 0.125
- proj_bias: bfloat16 [512], replicated, may hold values from -3 to 3
Outputs:
- layer_out: bfloat16 [32768, 512], P(('fsdp', 'tp'))
- input_grad: bfloat16 [32768, 512], P(('fsdp', 'tp'))
- first_gain_grad: float32 [512], replicated
- first_shift_grad: float32 [512], replicated
- qkv_weight_grad: float32 [512, 3, 512], P('fsdp', None, 'tp')
- qv_bias_grad: float32 [2, 512], replicated
- out_weight_grad: float32 [512, 512], P('tp', 'fsdp')
- out_bias_grad: float32 [512], replicated
- second_gain_grad: float32 [512], replicated
- second_shift_grad: float32 [512], replicated
- fc_weight_grad: float32 [512, 2048], P('fsdp', 'tp')
- fc_bias_grad: float32 [2048], replicated
- proj_weight_grad: float32 [2048, 512], P('tp', 'fsdp')
- proj_bias_grad: float32 [512], replicated
Inputs may be any that keep to these rules, and one draw needn't show every extreme that they name: `segments`: along each sequence the numbers start at 1 and rise by one from document to document; each document has 200 to 2000 tokens, and in one sequence every document has exactly 200; 0 marks padding, which only follows the last whole document of a sequence.
All inputs are finite; a program needn't handle non-finite values.
Results may differ from a plain program's by a relative error of at most 0.018.
The roundings to bfloat16 on the way count: a program that leaves them out, or rounds other values in their place, can miss the bound.
Values may be sent and summed in bfloat16 or wider, within the bound.
A program may use at most 128 MiB of HBM per device.

v0:
```python
import functools

import jax
import jax.numpy as jnp
from jax import lax
from jax.experimental import pallas as pl
from jax.experimental.pallas import tpu as pltpu
from jax.sharding import PartitionSpec as P

HD = 64
VMEM_LIMIT = 60 << 20
epsilon = 1e-05
gelu_slope = 1.702


def layer_norm(values_in, gain_vec, shift_vec):
    mean_row = jnp.mean(values_in, axis=-1, keepdims=True)
    centred = values_in - mean_row
    inverse = lax.rsqrt(jnp.mean(centred * centred, axis=-1, keepdims=True) + epsilon)
    normed = centred * inverse
    return (normed * gain_vec + shift_vec, normed, inverse)


def norm_back(grad_out, normed, inverse, gain_vec):
    scaled = grad_out * gain_vec
    grad_in = inverse * (
        scaled
        - jnp.mean(scaled, axis=-1, keepdims=True)
        - normed * jnp.mean(scaled * normed, axis=-1, keepdims=True)
    )
    return (grad_in, jnp.sum(grad_out * normed, axis=0), jnp.sum(grad_out, axis=0))


f32 = jnp.float32
bf16 = jnp.bfloat16
LOG2E = 1.4426950408889634
BLOCK = 512
TRANSPOSED = (((1,), (1,)), ((), ()))


def dot_t(left, right):
    return lax.dot_general(left, right, TRANSPOSED, preferred_element_type=f32)


def dot_n(left, right):
    return jnp.dot(left, right, preferred_element_type=f32)


def three_parts(value):
    top = value.astype(bf16)
    rest = value - top.astype(f32)
    mid = rest.astype(bf16)
    return top, mid, (rest - mid.astype(f32)).astype(bf16)


def diagonal_mask(seg_ref, row_at, size):
    key_pos = lax.broadcasted_iota(jnp.int32, (size, 1), 0)
    query_pos = lax.broadcasted_iota(jnp.int32, (1, size), 1)
    here = seg_ref.shape[2]
    seg = seg_ref[row_at // here, 0:1, pl.ds(pl.multiple_of(lax.rem(row_at, here), size), size)]
    first = jnp.where(seg == 0, query_pos, 0)
    return (key_pos >= first) & (key_pos <= query_pos)


def attend_kernel(
    low_ref, qa_ref, ka_ref, vt_ref, start_ref, out_ref, qb_ref, s0, s1, a0, a1, *, size, blocks
):
    score_bufs, acc_bufs = (s0, s1), (a0, a1)
    heads = range(qa_ref.shape[0])
    lane = lax.broadcasted_iota(jnp.int32, (size, 128), 1)

    def query_block(i, carry):
        row_at = pl.multiple_of(i * size, size)

        def score(h, j, top, diag):
            keys = ka_ref[h, pl.ds(pl.multiple_of(j * size, size), size), :]
            s = dot_t(keys, qa_ref[h, pl.ds(row_at, size), :])
            if diag:
                s = jnp.where(diagonal_mask(start_ref, row_at, size), s, -3e38)
            score_bufs[h][...] = s
            col_max = jnp.max(s, axis=0, keepdims=True)
            return col_max if top is None else jnp.maximum(top, col_max)

        def gather_values(h, j, old, new, first):
            p = jnp.exp2(score_bufs[h][...] * LOG2E - new * LOG2E).astype(bf16)
            part = dot_n(vt_ref[h, :, pl.ds(pl.multiple_of(j * size, size), size)], p)
            if first:
                acc_bufs[h][...] = part
            else:
                acc_bufs[h][...] = acc_bufs[h][...] * jnp.exp2((old - new) * LOG2E) + part

        low = low_ref[i, 0]
        m0 = score(0, i, None, True)
        m1 = score(1, i, None, True)
        gather_values(0, i, None, m0, True)
        m0n = score(0, jnp.minimum(low, i), m0, False)
        gather_values(1, i, None, m1, True)

        def body(j, c):
            m0, m0n, m1 = c
            m1n = score(1, j, m1, False)
            gather_values(0, j, m0, m0n, False)
            m0nn = score(0, jnp.minimum(j + 1, blocks - 1), m0n, False)
            gather_values(1, j, m1, m1n, False)
            return m0n, m0nn, m1n

        m0, _, m1 = lax.fori_loop(low, i, body, (m0, m0n, m1))
        for h, top in ((0, m0), (1, m1)):
            total = acc_bufs[h][64:65, :]
            out = acc_bufs[h][0:64, :] / total
            rows = qa_ref[h, pl.ds(row_at, size), :]
            live = jnp.where(rows[:, 64:65].astype(f32) != 0.0, 1.0, 0.0)
            out_ref[pl.ds(row_at, size), 64 * h : 64 * h + 64] = (out.T * live).astype(out_ref.dtype)
            norm = jnp.broadcast_to(-(top + jnp.log(total)), (8, size)).T[:, 0:1]
            n0, n1, n2 = three_parts(norm)
            rows = jnp.where(lane == 96, n0, jnp.where(lane == 97, n1, jnp.where(lane == 98, n2, rows)))
            qb_ref[h, pl.ds(row_at, size), :] = rows
        return carry

    lax.fori_loop(0, blocks, query_block, 0)


def attend(low, qa, ka, vt, start, size):
    heads, rows, _ = qa.shape
    vmem = pl.BlockSpec(memory_space=pltpu.VMEM)
    return pl.pallas_call(
        functools.partial(attend_kernel, size=size, blocks=rows // size),
        grid_spec=pltpu.PrefetchScalarGridSpec(
            num_scalar_prefetch=0,
            grid=(),
            in_specs=[pl.BlockSpec(memory_space=pltpu.SMEM)] + [vmem] * 4,
            out_specs=[vmem] * 2,
            scratch_shapes=[pltpu.VMEM((size, size), f32)] * heads
            + [pltpu.VMEM((vt.shape[1], size), f32)] * heads,
        ),
        out_shape=[
            jax.ShapeDtypeStruct((rows, HD * heads), bf16),
            jax.ShapeDtypeStruct(qa.shape, bf16),
        ],
        compiler_params=pltpu.CompilerParams(vmem_limit_bytes=VMEM_LIMIT),
        cost_estimate=pl.CostEstimate(
            flops=14 * rows * rows * HD * heads, bytes_accessed=8 << 20, transcendentals=rows * rows
        ),
        name="attend",
    )(low, qa, ka, vt, start)


def attend_back_kernel(
    low_ref, qb_ref, ka_ref, va_ref, kt_ref, g_ref, o_ref, start_ref, grad_ref,
    ga_ref, dk_ref, dv_ref, q0, q1, *, size, blocks
):
    query_accs = (q0, q1)
    lane = lax.broadcasted_iota(jnp.int32, (size, 64), 1)

    def query_block(i, carry):
        row_at = pl.multiple_of(i * size, size)
        g_rows = g_ref[pl.ds(row_at, size), :]
        product = g_rows.astype(f32) * o_ref[pl.ds(row_at, size), :].astype(f32)
        for h in range(2):
            cols = slice(64 * h, 64 * h + 64)
            n0, n1, n2 = three_parts(-jnp.sum(product[:, cols], axis=1, keepdims=True))
            zero = jnp.zeros((size, 64), bf16)
            extra = jnp.where(lane == 0, n0, jnp.where(lane == 1, n1, jnp.where(lane == 2, n2, zero)))
            ga_ref[h] = jnp.concatenate([g_rows[:, cols], extra], axis=1)

        def block(h, j, diag):
            key_at = pl.multiple_of(j * size, size)
            keys = ka_ref[h, pl.ds(key_at, size), :]
            q_rows = qb_ref[h, pl.ds(row_at, size), :]
            g_head = ga_ref[h]
            s = dot_t(keys, q_rows)
            if diag:
                s = jnp.where(diagonal_mask(start_ref, row_at, size), s, -3e38)
            p = jnp.exp2(s * LOG2E)
            dp = dot_t(va_ref[h, pl.ds(key_at, size), :], g_head)
            ds = (p * dp).astype(bf16)
            dv = dot_n(p.astype(bf16), g_head[:, 0:64])
            dk = dot_n(ds, q_rows[:, 0:64])
            dq = dot_n(kt_ref[h, :, pl.ds(key_at, size)], ds)
            if diag:
                dv_ref[h, pl.ds(key_at, size), :] = dv
                dk_ref[h, pl.ds(key_at, size), :] = dk
                query_accs[h][...] = dq
            else:
                dv_ref[h, pl.ds(key_at, size), :] += dv
                dk_ref[h, pl.ds(key_at, size), :] += dk
                query_accs[h][...] += dq

        block(0, i, True)
        block(1, i, True)

        def body(j, c):
            block(0, j, False)
            block(1, j, False)
            return c

        lax.fori_loop(low_ref[i, 0], i, body, 0)
        both = jnp.concatenate([query_accs[0][...], query_accs[1][...]], axis=0) * HD ** (-0.5)
        grad_ref[pl.ds(row_at, size), 0:128] = both.T.astype(bf16)
        return carry

    lax.fori_loop(0, blocks, query_block, 0)

    def finish(i, carry):
        row_at = pl.multiple_of(i * size, size)
        for ref, at in ((dk_ref, 128), (dv_ref, 256)):
            both = jnp.concatenate([ref[0, pl.ds(row_at, size), :], ref[1, pl.ds(row_at, size), :]], axis=1)
            grad_ref[pl.ds(row_at, size), at : at + 128] = both.astype(bf16)
        return carry

    lax.fori_loop(0, blocks, finish, 0)


def attend_back(low, qb, ka, va, kt, g, o, start, size):
    heads, rows, _ = qb.shape
    vmem = pl.BlockSpec(memory_space=pltpu.VMEM)
    return pl.pallas_call(
        functools.partial(attend_back_kernel, size=size, blocks=rows // size),
        grid_spec=pltpu.PrefetchScalarGridSpec(
            num_scalar_prefetch=0,
            grid=(),
            in_specs=[pl.BlockSpec(memory_space=pltpu.SMEM)] + [vmem] * 7,
            out_specs=vmem,
            scratch_shapes=[
                pltpu.VMEM((heads, size, 128), bf16),
                pltpu.VMEM((heads, rows, HD), f32),
                pltpu.VMEM((heads, rows, HD), f32),
            ]
            + [pltpu.VMEM((HD, size), f32)] * heads,
        ),
        out_shape=jax.ShapeDtypeStruct((rows, 3 * HD * heads), bf16),
        compiler_params=pltpu.CompilerParams(vmem_limit_bytes=VMEM_LIMIT),
        cost_estimate=pl.CostEstimate(
            flops=24 * rows * rows * HD * heads, bytes_accessed=16 << 20, transcendentals=rows * rows
        ),
        name="attend_back",
    )(low, qb, ka, va, kt, g, o, start)


MESH = pl.DeviceIdType.MESH


def greet(peers):
    barrier = pltpu.get_barrier_semaphore()
    for peer in peers:
        pl.semaphore_signal(barrier, inc=1, device_id=peer, device_id_type=MESH)
    pl.semaphore_wait(barrier, len(peers))


def push(source, target, send_sem, recv_sem, peer):
    copy = pltpu.make_async_remote_copy(
        src_ref=source,
        dst_ref=target,
        send_sem=send_sem,
        recv_sem=recv_sem,
        device_id=peer,
        device_id_type=MESH,
    )
    copy.start()
    return copy


def quad():
    me = lax.axis_index("tp")
    side = me + 1 - 2 * lax.rem(me, 2)
    across = lax.rem(me + 2, 4)
    far = lax.rem(side + 2, 4)
    return me, side, across, far


def comm_call(kernel, name, number, out_shape, in_specs, out_specs, scratch, moved, *operands):
    return pl.pallas_call(
        kernel,
        out_shape=out_shape,
        in_specs=in_specs,
        out_specs=out_specs,
        scratch_shapes=scratch,
        compiler_params=pltpu.CompilerParams(
            collective_id=number, has_side_effects=True, vmem_limit_bytes=VMEM_LIMIT
        ),
        cost_estimate=pl.CostEstimate(flops=0, bytes_accessed=moved, transcendentals=0),
        name=name,
    )(*operands)


def in_vmem():
    return pl.BlockSpec(memory_space=pltpu.VMEM)


def anywhere():
    return pl.BlockSpec(memory_space=pl.ANY)


def flipped(axis, mask):
    me, index, bit = lax.axis_index(axis), lax.axis_index(axis), 1
    while bit <= mask:
        if mask & bit:
            index = index + bit - 2 * bit * lax.rem(me // bit, 2)
        bit *= 2
    return index


def awaited(ref, send_sem, recv_sem, peer):
    return pltpu.make_async_remote_copy(ref, ref, send_sem, recv_sem, peer, MESH)


def hop_masks(size):
    hops, bit = [], size // 2
    while bit >= 1:
        hops.append((bit, [high + bit for high in range(0, size, 2 * bit)]))
        bit //= 2
    return hops


def enter_kernel(
    x_ref, par_ref, seg_ref, w0, w1, w2, w3,
    normed_ref, segs_ref, low_ref, qa_ref, ka_ref, va_ref, vt_ref, kt_ref, f0, f1,
    x_all, normed_s, qa_s, ka_s, va_s, vt_s, kt_s,
    sy, ry, ss, rs, sf, rf, sg, rg, sw, rw, own, own_w, outs, *, parts, size
):
    me, side, across, far = quad()
    rows = x_ref.shape[0]
    step = rows // parts
    shards = f0.shape[0]
    heads = qa_ref.shape[0]
    width = HD * heads
    shard = lax.axis_index("fsdp")
    hops = hop_masks(shards)
    greet(
        [{"tp": side}, {"tp": across}, {"tp": far}]
        + [{"fsdp": flipped("fsdp", bit)} for bit, _ in hops]
    )
    sent = []

    def rows_of(owner, part):
        return x_all.at[pl.ds(pl.multiple_of(owner * rows + part * step, step), step)]

    sources = (w0, w1, w2, w3)

    def block_of(g, index):
        if g == 0:
            return f0.at[index]
        at = sum(w.shape[1] for w in sources[1:g])
        return f1.at[index, :, pl.ds(at, sources[g].shape[1])]

    def send_hop(g, hop):
        bit, masks = hops[hop]
        peer = {"fsdp": flipped("fsdp", bit)}
        if hop > 0:
            before, arrived = hops[hop - 1]
            for mask in arrived:
                block = block_of(g, flipped("fsdp", mask))
                awaited(block, sw.at[g, mask], rw.at[g, mask], {"fsdp": flipped("fsdp", before)}).wait_recv()
        for mask in masks:
            target = block_of(g, flipped("fsdp", mask - bit))
            block = sources[g] if mask == bit else target
            sent.append(push(block, target, sw.at[g, mask], rw.at[g, mask], peer))

    def end_hops(g):
        bit, arrived = hops[-1]
        for mask in arrived:
            block = block_of(g, flipped("fsdp", mask))
            awaited(block, sw.at[g, mask], rw.at[g, mask], {"fsdp": flipped("fsdp", bit)}).wait_recv()

    for k, peer in enumerate((across, far, side)):
        sent.append(push(seg_ref, segs_ref.at[me], sg.at[k], rg.at[k], {"tp": peer}))
    send_hop(0, 0)
    for part in range(parts):
        mine = x_ref.at[pl.ds(part * step, step)]
        sent.append(push(mine, rows_of(me, part), sy.at[part], ry.at[part], {"tp": across}))
    send_hop(0, 1)
    for g in (1, 2, 3):
        send_hop(g, 0)
    for part in range(parts):
        mine = x_ref.at[pl.ds(part * step, step)]
        sent.append(push(mine, rows_of(me, part), ss.at[part], rs.at[part], {"tp": side}))
    kept = [
        pltpu.make_async_copy(x_ref, x_all.at[pl.ds(pl.multiple_of(me * rows, rows), rows)], own.at[0]),
        pltpu.make_async_copy(seg_ref, segs_ref.at[me], own.at[1]),
    ] + [pltpu.make_async_copy(source, block_of(g, shard), own_w.at[g]) for g, source in enumerate(sources)]
    for copy in kept:
        copy.start()
    waves = sorted(
        ((hop + g, g, hop) for hop in range(1, len(hops)) for g in range(4)), key=lambda w: (w[0], w[1])
    )
    for _, g, hop in waves[1:2]:
        send_hop(g, hop)
    for k, peer in enumerate((across, far, side)):
        awaited(segs_ref.at[peer], sg.at[k], rg.at[k], {"tp": peer}).wait_recv()
    for part in range(parts):
        awaited(rows_of(side, part), ss.at[part], rs.at[part], {"tp": side}).wait_recv()
    for copy in kept:
        copy.wait()
    gain, shift = par_ref[8:9, :], par_ref[9:10, :]

    def norm(owner, part):
        span = pl.ds(pl.multiple_of(owner * rows + part * step, step), step)
        x = x_all[span, :].astype(f32)
        centred = x - jnp.mean(x, axis=-1, keepdims=True)
        inverse = lax.rsqrt(jnp.mean(centred * centred, axis=-1, keepdims=True) + epsilon)
        normed_s[span, :] = (centred * inverse * gain + shift).astype(bf16)

    def norm_near(k, carry):
        norm(me + lax.rem(k, 2) * (side - me), k // 2)
        return carry

    lax.fori_loop(0, 2 * parts, norm_near, 0)
    whole = [segs_ref[n, 0:1, :] for n in range(4)]
    for n in range(4 * rows // size):
        at = n * size
        first = whole[at // rows][:, at % rows : at % rows + 1]
        before = sum(
            jnp.sum(jnp.where((seg > 0) & (seg < first), 1.0, 0.0), axis=1, keepdims=True) for seg in whole
        )
        block = jnp.where(first == 0, n * size, before.astype(jnp.int32)) // size
        low_ref[n : n + 1, :] = jnp.broadcast_to(block, (1, low_ref.shape[1]))
    for _, g, hop in waves[2:]:
        send_hop(g, hop)
    end_hops(0)
    bias_at = pl.ds(pl.multiple_of(me * width, width), width)
    query_bias = par_ref[10:11, bias_at]
    value_bias = par_ref[11:12, bias_at]
    number = lax.broadcasted_iota(jnp.int32, (step, 64), 1)
    number_f = number.astype(f32)
    key_ones = (number >= 32) & (number < 35)
    value_tail = jnp.where(number < 3, 1.0, 0.0).astype(bf16)
    ones_row = jnp.where(lax.broadcasted_iota(jnp.int32, (16, step), 0) == 0, 1.0, 0.0).astype(bf16)

    def copies_out(owner, part):
        row = pl.multiple_of(owner * rows + part * step, step)
        slot = owner * parts + part
        span = pl.ds(row, step)
        pairs = [(normed_s.at[span], normed_ref.at[span])]
        for a, b in ((qa_s, qa_ref), (ka_s, ka_ref), (va_s, va_ref)):
            pairs.append((a.at[:, span, :], b.at[:, span, :]))
        for a, b in ((vt_s, vt_ref), (kt_s, kt_ref)):
            pairs.append((a.at[:, :, span], b.at[:, :, span]))
        return [pltpu.make_async_copy(a, b, outs.at[n, slot]) for n, (a, b) in enumerate(pairs)]

    def compute(owner, part):
        row = pl.multiple_of(owner * rows + part * step, step)
        span = pl.ds(row, step)
        normed = normed_s[span, :]
        weights = f0[...].reshape(shards * f0.shape[1], 3 * width)
        projected = dot_n(normed, weights)
        queries = ((projected[:, 0:width] + query_bias).astype(bf16).astype(f32) * HD ** (-0.5)).astype(bf16)
        keys = projected[:, width : 2 * width].astype(bf16)
        values = (projected[:, 2 * width : 3 * width] + value_bias).astype(bf16)
        seg = segs_ref[owner, 0:1, pl.ds(pl.multiple_of(part * step, step), step)].astype(f32)
        seg = jnp.broadcast_to(seg, (8, step)).T[:, 0:1]
        same = (seg == number_f) & (number < 32)
        other = jnp.where(same | (number > 31), 0.0, -1e30).astype(bf16)
        key_tail = jnp.where(same | key_ones, 1.0, 0.0).astype(bf16)
        for h in range(heads):
            cols = slice(HD * h, HD * h + HD)
            qa_s[h, span, :] = jnp.concatenate([queries[:, cols], other], axis=1)
            ka_s[h, span, :] = jnp.concatenate([keys[:, cols], key_tail], axis=1)
            va_s[h, span, :] = jnp.concatenate([values[:, cols], value_tail], axis=1)
            turned = jnp.concatenate([values[:, cols], keys[:, cols]], axis=1).astype(f32).T.astype(bf16)
            vt_s[h, 0:64, span] = turned[0:64, :]
            vt_s[h, 64:80, span] = ones_row
            kt_s[h, :, span] = turned[64:128, :]
        for copy in copies_out(owner, part):
            copy.start()

    def work(k, carry):
        distant = k // (2 * parts)
        part = lax.rem(k // 2, parts)
        second = lax.rem(k, 2)

        @pl.when((distant == 0) & (second == 0))
        def _():
            here = rows_of(across, part)
            awaited(here, sy.at[part], ry.at[part], {"tp": across}).wait_recv()
            push(here, here, sf.at[part], rf.at[part], {"tp": side})

        @pl.when((distant == 1) & (second == 1))
        def _():
            awaited(rows_of(far, part), sf.at[part], rf.at[part], {"tp": side}).wait_recv()

        @pl.when(distant == 1)
        def _():
            norm(across + second * (far - across), part)

        first = me + distant * (across - me)
        compute(first + second * (side - me + distant * (far - across - side + me)), part)
        return carry

    lax.fori_loop(0, 4 * parts, work, 0)
    for g in (1, 2, 3):
        end_hops(g)

    def drain(k, carry):
        for copy in copies_out(k // parts, lax.rem(k, parts)):
            copy.wait()
        return carry

    lax.fori_loop(0, 4 * parts, drain, 0)
    for part in range(parts):
        awaited(rows_of(across, part), sf.at[part], rf.at[part], {"tp": side}).wait_send()
    for copy in sent:
        copy.wait_send()


def enter(x, params, segments, weights, size, number, parts=4):
    rows, width = x.shape
    seq_rows = 4 * rows
    shards = lax.axis_size("fsdp")
    heads = weights[0].shape[1] // (3 * HD)
    dma = pltpu.SemaphoreType.DMA
    wide = (heads, seq_rows, 128)
    shard_rows = weights[0].shape[0]
    full = [(shards, *weights[0].shape), (shards, shard_rows, sum(w.shape[1] for w in weights[1:]))]
    shapes = [(seq_rows, width), wide, wide, wide, (heads, 80, seq_rows), (heads, 64, seq_rows)]
    made = [jax.ShapeDtypeStruct(s, bf16) for s in shapes]
    return comm_call(
        functools.partial(enter_kernel, parts=parts, size=size),
        "enter",
        number,
        [made[0], jax.ShapeDtypeStruct((4, *segments.shape), segments.dtype)]
        + [jax.ShapeDtypeStruct((seq_rows // size, 128), jnp.int32)]
        + made[1:]
        + [jax.ShapeDtypeStruct(s, bf16) for s in full],
        [in_vmem()] * 7,
        [anywhere(), in_vmem(), in_vmem()] + [anywhere()] * 5 + [in_vmem(), anywhere()],
        [pltpu.VMEM((seq_rows, width), bf16)]
        + [pltpu.VMEM(s, bf16) for s in shapes]
        + [dma((parts,))] * 6
        + [dma((3,))] * 2
        + [dma((4, shards))] * 2
        + [dma((2,)), dma((4,)), dma((6, 4 * parts))],
        60 << 20,
        x,
        params,
        segments,
        *weights,
    )


def middle_kernel(
    seq_out, own_ref, passed_ref, x_ref, g_ref, seg_ref, par_ref,
    layer_ref, resid_ref, seq_ref, kept_ref, over_ref, sums_ref,
    attn_ref, fc_ref, pj_ref, ow_ref, attn_cat, ow_cat, act_s, gp_s, in_s, in_t, g_t, low_t, ga_s, out_acc, gn_acc,
    fc_g, pj_g, ow_g, fc_box, pj_box, ow_box,
    sems, rems, ws, wr, sa, ra, sv, rv, own_sem, *, parts
):
    me, side, across, far = quad()
    greet([{"tp": side}, {"tp": across}, {"tp": far}])
    peers = {1: side, 2: across, 3: far}
    rows = x_ref.shape[0]
    step = rows // parts
    lanes = ow_ref.shape[2]
    sums_ref[...] = jnp.zeros_like(sums_ref)

    def own_rows(who, part):
        return seq_out.at[pl.ds(pl.multiple_of(who * rows + part * step, step), step)]

    def send_rows(part, carry):
        here = pl.ds(pl.multiple_of(part * step, step), step)
        for k in (3, 2, 1):
            push(own_rows(peers[k], part), attn_ref.at[k, here], sa.at[k, part], ra.at[k, part], {"tp": peers[k]})
        return carry

    lax.fori_loop(0, parts, send_rows, 0)
    sent, kept, at = [], [], 0
    for n, full in enumerate((fc_ref, pj_ref, ow_ref)):
        cols = pl.ds(at, full.shape[2])
        at += full.shape[2]
        for k, source in ((0, own_ref), (2, passed_ref)):
            block = source.at[:, cols]
            sent.append(push(block, full.at[k + 1], sv.at[k // 2, n], rv.at[k // 2, n], {"tp": side}))
            kept.append(pltpu.make_async_copy(block, full.at[k], own_sem.at[2 * n + k // 2]))
    mine = seq_out.at[pl.ds(pl.multiple_of(me * rows, rows), rows)]
    kept.append(pltpu.make_async_copy(mine, attn_ref.at[0], own_sem.at[6]))
    for copy in kept:
        copy.start()
    for copy in kept:
        copy.wait()
    for copy in sent:
        copy.wait()
    for p in range(4):
        ow_cat[:, p * lanes : (p + 1) * lanes] = ow_ref[p]

    def owner(t):
        near = me + lax.rem(t, 2) * (1 - 2 * lax.rem(me, 2))
        return lax.rem(near + 2 * (t // 2), 4)

    def add_row(row, value):
        at = pl.ds(row, 1)
        sums_ref[at, :] = sums_ref[at, :] + jnp.sum(value, axis=0, keepdims=True)

    def landing(who, part):
        return seq_ref.at[pl.ds(pl.multiple_of(who * rows + part * step, step), step)]

    def row_block(part, carry):
        here = pl.ds(pl.multiple_of(part * step, step), step)
        for k in (1, 2, 3):
            awaited(attn_ref.at[k, here], sa.at[k, part], ra.at[k, part], {"tp": peers[k]}).wait_recv()
        attn = jnp.concatenate([attn_ref[p, here, :] for p in range(4)], axis=1)
        attn_cat[here, :] = attn
        hidden = x_ref[here, :].astype(f32) + dot_t(attn, ow_cat[...]) + par_ref[0:1, :]
        gain = par_ref[1:2, :]
        normed, hat, inverse = layer_norm(hidden, gain, par_ref[2:3, :])
        in_s[...] = normed.astype(bf16)
        in_t[:, here] = normed.T.astype(bf16)
        grad = g_ref[here, :]
        g_t[:, here] = grad.astype(f32).T.astype(bf16)
        out_acc[...] = hidden + par_ref[3:4, :]
        gn_acc[...] = jnp.zeros_like(gn_acc)

        def hidden_block(t, c):
            bias_at = 4 + owner(t)
            pre = dot_n(in_s[...], fc_ref[t]) + par_ref[pl.ds(bias_at, 1), :]
            gate = jax.nn.sigmoid(gelu_slope * pre)
            raised = pre * gate
            act = raised.astype(bf16)
            act_s[t, here, :] = act
            out_acc[...] += dot_t(act, pj_ref[t])
            grad_act = dot_n(g_ref[here, :], pj_ref[t])
            grad_pre = (grad_act * (gate + gelu_slope * raised * (1.0 - gate))).astype(bf16)
            gp_s[t, here, :] = grad_pre
            add_row(bias_at, grad_pre.astype(f32))
            gn_acc[...] += dot_t(grad_pre, fc_ref[t])
            return c

        lax.fori_loop(0, 4, hidden_block, 0)
        layer_ref[here, :] = out_acc[...].astype(bf16)
        grad_in, gain_part, shift_part = norm_back(gn_acc[...], hat, inverse, gain)
        grad_hidden = grad.astype(f32) + grad_in
        resid_ref[here, :] = grad_hidden
        low = grad_hidden.astype(bf16)
        low_t[:, here] = grad_hidden.T.astype(bf16)
        sums_ref[1:2, :] += gain_part[None]
        sums_ref[2:3, :] += shift_part[None]
        add_row(0, low.astype(f32))
        add_row(3, grad.astype(f32))
        seg = jnp.broadcast_to(seg_ref[0:1, here].astype(f32), (8, step)).T[:, 0:1]
        live = jnp.where(seg != 0.0, 1.0, 0.0)
        grad_attn = (dot_n(low, ow_cat[...]).astype(bf16).astype(f32) * live).astype(bf16)
        for k in (1, 2, 3):
            ga_s[k, here, :] = grad_attn[:, k * lanes : (k + 1) * lanes]
        seq_ref[pl.ds(pl.multiple_of(me * rows + part * step, step), step), :] = grad_attn[:, 0:lanes]
        for k in (3, 2, 1):
            push(ga_s.at[k, here], landing(me, part), sems.at[k, part], rems.at[k, part], {"tp": peers[k]})
        return carry

    lax.fori_loop(0, parts, row_block, 0)
    width = out_acc.shape[1]
    tall = 128

    def out_block(n, carry):
        at = pl.ds(pl.multiple_of(n * tall, tall), tall)
        grad = dot_n(low_t[at, :], attn_cat[...]).astype(bf16)
        for p in range(4):
            ow_g[p, at, :] = grad[:, p * lanes : (p + 1) * lanes]
        return carry

    lax.fori_loop(0, width // tall, out_block, 0)
    triples = ((fc_g, fc_box), (pj_g, pj_box), (ow_g, ow_box))

    def fold(n, b):
        grad, box = triples[n]
        return grad.at[2 * b + 1], box.at[b], ws.at[n, b], wr.at[n, b], {"tp": side}

    for b in (1, 0):
        push(*fold(2, b))

    def slice_block(u, carry):
        t = 3 - 2 * u + 3 * (u // 2)

        def fc_block(n, c):
            at = pl.ds(pl.multiple_of(n * tall, tall), tall)
            fc_g[t, at, :] = dot_n(in_t[at, :], gp_s[t]).astype(bf16)
            pj_g[t, at, :] = dot_n(g_t[at, :], act_s[t]).astype(bf16)
            return c

        lax.fori_loop(0, width // tall, fc_block, 0)
        for b in (1, 0):

            @pl.when(u == 1 - b)
            def _():
                push(*fold(0, b))
                push(*fold(1, b))

        return carry

    lax.fori_loop(0, 4, slice_block, 0)
    for b, target in ((1, over_ref), (0, kept_ref)):
        at = 0
        for n, (grad, box) in enumerate(triples):
            cols = slice(at, at + grad.shape[2])
            at += grad.shape[2]
            awaited(box.at[b], ws.at[n, b], wr.at[n, b], {"tp": side}).wait_recv()
            target[:, cols] = (grad[2 * b].astype(f32) + box[b].astype(f32)).astype(bf16)

    def drain(part, carry):
        here = pl.ds(pl.multiple_of(part * step, step), step)
        for k in (1, 2, 3):
            peer = {"tp": peers[k]}
            awaited(landing(peers[k], part), sems.at[k, part], rems.at[k, part], peer).wait_recv()
            awaited(ga_s.at[k, here], sems.at[k, part], rems.at[k, part], peer).wait_send()
            awaited(own_rows(peers[k], part), sa.at[k, part], ra.at[k, part], peer).wait_send()
        return carry

    lax.fori_loop(0, parts, drain, 0)
    for n, (grad, box) in enumerate(triples):
        for b in (1, 0):
            awaited(grad.at[2 * b + 1], ws.at[n, b], wr.at[n, b], {"tp": side}).wait_send()


def middle(attn, own, passed, x, grad, segments, params, hidden, number, parts=4):
    rows, lanes = x.shape[0], attn.shape[1]
    width = x.shape[1]
    fc = pj = (4, width, hidden)
    ow = (4, width, lanes)
    step = rows // parts
    dma = pltpu.SemaphoreType.DMA
    total = 2 * hidden + lanes
    low, wide = bf16, f32
    scratch = [
        ((4, rows, lanes), low), (fc, low), (pj, low), (ow, low),
        ((rows, width), low), ((width, 4 * lanes), low),
        ((4, rows, hidden), low), ((4, rows, hidden), low),
        ((step, width), low), ((width, rows), low), ((width, rows), low), ((width, rows), low),
        ((4, rows, lanes), low), ((step, width), wide), ((step, width), wide),
        (fc, low), (pj, low), (ow, low),
        ((2, *fc[1:]), low), ((2, *pj[1:]), low), ((2, *ow[1:]), low),
    ]
    outs = [
        ((rows, width), low), ((rows, width), wide), ((4 * rows, lanes), low),
        ((width, total), low), ((width, total), low), ((8, width), wide),
    ]
    return comm_call(
        functools.partial(middle_kernel, parts=parts),
        "middle",
        number,
        [jax.ShapeDtypeStruct(s, d) for s, d in outs],
        [in_vmem(), anywhere(), anywhere()] + [in_vmem()] * 4,
        [in_vmem()] * 6,
        [pltpu.VMEM(s, d) for s, d in scratch]
        + [dma((4, parts)), dma((4, parts)), dma((3, 2)), dma((3, 2))]
        + [dma((4, parts)), dma((4, parts)), dma((2, 3)), dma((2, 3)), dma((7,))],
        60 << 20,
        attn,
        own,
        passed,
        x,
        grad,
        segments,
        params,
    )


def leave_kernel(
    grad_ref, normed_in, w_ref, kept_ref, came_ref, early_ref, x_in, gain_ref, resid_in,
    input_ref, s0, s1, s2, s3, early_out, late_out,
    rows_ref, far_out, own_out, sum_buf, side_far, side_own, over, dw_acc, cols_ref,
    late_ref, early_mid, late_mid, early_one, early_two, late_one, late_two,
    normed_ref, x_ref, resid_ref, loads,
    sa, ra, sb, rb, sy, ry, sw, rw, se, re, sl, rl, se2, re2, sl2, rl2, *bufs, parts, hops
):
    me, side, across, far = quad()
    rows = rows_ref.shape[0]
    step = rows // parts
    shard, shards = lax.axis_index("fsdp"), early_two.shape[0]
    pairs = ((normed_in, normed_ref), (x_in, x_ref), (resid_in, resid_ref))
    loading = [pltpu.make_async_copy(a, b, loads.at[n]) for n, (a, b) in enumerate(pairs)]
    for copy in loading:
        copy.start()
    barrier = pltpu.get_barrier_semaphore()
    for peer in (side, across, far):
        pl.semaphore_signal(barrier, inc=1, device_id={"tp": peer}, device_id_type=MESH)

    def other(k):
        return {"fsdp": lax.rem(shard + k, shards)}

    def signal(k, carry):
        pl.semaphore_signal(barrier, inc=1, device_id=other(k), device_id_type=MESH)
        return carry

    lax.fori_loop(1, shards, signal, 0)
    pl.semaphore_wait(barrier, 3 + shards - 1)
    count = len(hops)
    outs = (s0, s1, s2, s3)
    current = bufs[0:4]
    boxes = [bufs[4 + g * count : 4 + (g + 1) * count] for g in range(4)]
    keeps = [bufs[4 + 4 * count + g * (count - 1) : 4 + 4 * count + (g + 1) * (count - 1)] for g in range(4)]
    sent = []

    def begin(g):
        at = sum(c.shape[3] for c in current[0:g])
        cols = slice(at, at + current[g].shape[3])
        total = kept_ref[:, :, :, cols].astype(f32) + came_ref[:, :, :, cols].astype(f32)
        current[g][...] = total.astype(bf16)

    def hop_parts(g, k):
        axis, bit = hops[k]
        source = current[g] if k == 0 else keeps[g][k - 1]
        half = lax.rem(lax.axis_index(axis) // bit, 2)
        return {axis: flip(axis, bit)}, source, half, boxes[g][k]

    def hop_send(g, k):
        peer, source, half, box = hop_parts(g, k)
        sent.append(push(source.at[:, 1 - half], box, sw.at[g, k], rw.at[g, k], peer))

    def hop_add(g, k):
        peer, source, half, box = hop_parts(g, k)
        awaited(box, sw.at[g, k], rw.at[g, k], peer).wait_recv()
        if k == count - 1:
            outs[g][...] = source[0, half].astype(f32) + box[0].astype(f32)
        else:
            target = keeps[g][k]
            for n in range(box.shape[0]):
                total = source[n, half].astype(f32) + box[n].astype(f32)
                target[n // 2, n % 2] = total.astype(bf16)
            hop_send(g, k + 1)

    def tp_send(value, box, send, recv):
        box[me] = value[...]
        for k, peer in enumerate((side, across, far)):
            sent.append(push(value, box.at[me], send.at[k], recv.at[me], {"tp": peer}))

    def tp_sum(value, box, send, recv):
        for k, peer in enumerate((side, across, far)):
            awaited(box.at[peer], send.at[k], recv.at[peer], {"tp": peer}).wait_recv()
        value[...] = box[0] + box[1] + box[2] + box[3]

    def fsdp_send(value, box, send, recv):
        box[shard] = value[...]

        def give(k, carry):
            push(value, box.at[shard], send.at[k], recv.at[shard], other(k))
            return carry

        lax.fori_loop(1, shards, give, 0)

    def fsdp_sum(value, target, box, send, recv):
        def take(k, carry):
            peer = lax.rem(shard + k, shards)
            copy = awaited(box.at[peer], send.at[k], recv.at[peer], other(k))
            copy.wait_recv()
            copy.wait_send()
            return carry

        lax.fori_loop(1, shards, take, 0)
        target[...] = lax.fori_loop(1, shards, lambda n, total: total + box[n], box[0])

    def span(owner, part):
        return pl.ds(pl.multiple_of(owner * rows + part * step, step), step)

    def piece(part):
        return pl.ds(pl.multiple_of(part * step, step), step)

    def partial(owner, part):
        return dot_t(grad_ref[span(owner, part), :], w_ref[...])

    def give_far(part, carry):
        here = piece(part)
        far_out[here, :] = partial(far, part).astype(bf16)
        push(far_out.at[here], side_far.at[here], sa.at[part], ra.at[part], {"tp": side})
        return carry

    def give_over(part, carry):
        here = piece(part)
        mine = partial(across, part)
        awaited(side_far.at[here], sa.at[part], ra.at[part], {"tp": side}).wait_recv()
        sum_buf[here, :] = (mine + side_far[here, :].astype(f32)).astype(bf16)
        push(sum_buf.at[here], over.at[here], sy.at[part], ry.at[part], {"tp": across})
        return carry

    def give_own(part, carry):
        here = piece(part)
        own_out[here, :] = partial(side, part).astype(bf16)
        push(own_out.at[here], side_own.at[here], sb.at[part], rb.at[part], {"tp": side})
        return carry

    def take_own(part, carry):
        here = piece(part)
        mine = partial(me, part)
        awaited(side_own.at[here], sb.at[part], rb.at[part], {"tp": side}).wait_recv()
        rows_ref[here, :] = mine + side_own[here, :].astype(f32)
        return carry

    gain = gain_ref[8:9, :]

    def take_over(part, carry):
        here = piece(part)
        x = x_ref[here, :].astype(f32)
        centred = x - jnp.mean(x, axis=-1, keepdims=True)
        inverse = lax.rsqrt(jnp.mean(centred * centred, axis=-1, keepdims=True) + epsilon)
        normed = centred * inverse
        awaited(over.at[here], sy.at[part], ry.at[part], {"tp": across}).wait_recv()
        grad = rows_ref[here, :] + over[here, :].astype(f32)
        grad_in, gain_part, shift_part = norm_back(grad, normed, inverse, gain)
        input_ref[here, :] = (resid_ref[here, :] + grad_in).astype(bf16)
        late_ref[0:1, :] += gain_part[None]
        late_ref[1:2, :] += shift_part[None]
        return carry

    def drain(part, carry):
        here = piece(part)
        awaited(far_out.at[here], sa.at[part], ra.at[part], {"tp": side}).wait_send()
        awaited(own_out.at[here], sb.at[part], rb.at[part], {"tp": side}).wait_send()
        awaited(sum_buf.at[here], sy.at[part], ry.at[part], {"tp": across}).wait_send()
        return carry

    chunk = 512
    steps = grad_ref.shape[0] // chunk
    dw_acc[...] = jnp.zeros_like(dw_acc)
    cols_ref[...] = jnp.zeros_like(cols_ref)
    ones = jnp.ones((8, chunk), bf16)

    def weight_grad(n, carry):
        at = pl.ds(pl.multiple_of(n * chunk, chunk), chunk)
        g = grad_ref[at, :]
        dw_acc[...] += lax.dot_general(
            normed_ref[at, :], g, (((0,), (0,)), ((), ())), preferred_element_type=f32
        )
        cols_ref[...] += dot_n(ones, g)
        return carry

    tp_send(early_ref, early_one, se, re)
    lax.fori_loop(0, parts, give_far, 0)
    for g in (0, 1):
        begin(g)
        hop_send(g, 0)
    lax.fori_loop(0, parts, give_over, 0)
    begin(2)
    for copy in loading:
        copy.wait()
    lax.fori_loop(0, steps // 2, weight_grad, 0)
    hop_add(0, 0)
    lax.fori_loop(steps // 2, steps, weight_grad, 0)
    current[3][...] = dw_acc[...].astype(bf16).reshape(current[3].shape)
    hop_send(3, 0)
    hop_send(2, 0)
    tp_sum(early_mid, early_one, se, re)
    fsdp_send(early_mid, early_two, se2, re2)
    hop_add(1, 0)
    late_ref[...] = jnp.zeros_like(late_ref)
    wide = cols_ref.shape[1] // 3
    qv_at = pl.ds(pl.multiple_of(me * wide, wide), wide)
    late_ref[2:3, qv_at] = cols_ref[0:1, 0:wide]
    late_ref[3:4, qv_at] = cols_ref[0:1, 2 * wide : 3 * wide]
    lax.fori_loop(0, parts, give_own, 0)
    turns = enumerate((0, 1, 3, 2))
    order = sorted((k + turn, turn, g, k) for turn, g in turns for k in range(count))
    order = [(g, k) for _, _, g, k in order if (g, k) not in ((0, 0), (1, 0))]
    lax.fori_loop(0, parts, take_own, 0)
    taken = {len(order) * share // 10: span for share, span in ((6, (0, 2)), (7, (2, 3)), (9, (3, 4)))}
    for n, (g, k) in enumerate(order):
        if n in taken:
            first, last = taken[n]
            lax.fori_loop(first * parts // 4, last * parts // 4, take_over, 0)
        if n == len(order) - 1:
            tp_send(late_ref, late_one, sl, rl)
        hop_add(g, k)
    fsdp_sum(early_mid, early_out, early_two, se2, re2)
    tp_sum(late_mid, late_one, sl, rl)
    fsdp_send(late_mid, late_two, sl2, rl2)
    lax.fori_loop(0, parts, drain, 0)
    fsdp_sum(late_mid, late_out, late_two, sl2, rl2)
    for copy in sent:
        copy.wait_send()


def leave(grad, normed, w, kept, came, widths, early, x, gain, resid, number, parts=4):
    rows, width = grad.shape[0] // 4, w.shape[0]
    dma = pltpu.SemaphoreType.DMA
    hops = bits_of("fsdp")
    count = len(hops)
    shards = lax.axis_size("fsdp")
    shard = width // shards
    widths = [*widths, grad.shape[1]]
    split = (shards // 2, 2, shard)
    current = [pltpu.VMEM((*split, n), bf16) for n in widths]
    boxes = [pltpu.VMEM((shards >> (k + 1), shard, n), bf16) for n in widths for k in range(count)]
    keeps = [pltpu.VMEM((shards >> (k + 2), 2, shard, n), bf16) for n in widths for k in range(count - 1)]
    late = (4, width)
    return comm_call(
        functools.partial(leave_kernel, parts=parts, hops=hops),
        "leave",
        number,
        [jax.ShapeDtypeStruct((rows, width), bf16)]
        + [jax.ShapeDtypeStruct((shard, n), f32) for n in widths]
        + [jax.ShapeDtypeStruct(early.shape, f32), jax.ShapeDtypeStruct(late, f32)],
        [in_vmem(), anywhere()] + [in_vmem()] * 4 + [anywhere(), in_vmem(), anywhere()],
        [in_vmem()] * 7,
        [pltpu.VMEM((rows, width), f32)]
        + [pltpu.VMEM((rows, width), bf16)] * 6
        + [pltpu.VMEM((width, grad.shape[1]), f32), pltpu.VMEM((8, grad.shape[1]), f32)]
        + [pltpu.VMEM(late, f32), pltpu.VMEM(early.shape, f32), pltpu.VMEM(late, f32)]
        + [pltpu.VMEM((n, *shape), f32) for shape in (early.shape, late) for n in (4, shards)]
        + [pltpu.VMEM(v.shape, v.dtype) for v in (normed, x, resid)]
        + [dma((3,))]
        + [dma((parts,))] * 6
        + [dma((4, count))] * 2
        + [dma((3,)), dma((4,))] * 2
        + [dma((shards,))] * 4
        + current
        + boxes
        + keeps,
        60 << 20,
        grad,
        normed,
        w,
        kept.reshape(*split, kept.shape[1]),
        came.reshape(*split, came.shape[1]),
        early,
        x,
        gain,
        resid,
    )


def finish_kernel(
    rows_in, fc_in, proj_in, out_in, qkv_in, early_in, late_in,
    rows_ref, fc_ref, proj_ref, out_ref, qkv_ref, qv_ref, *vectors
):
    rows_ref[...] = rows_in[...]
    fc_ref[...] = fc_in[...]
    proj_ref[...] = proj_in[...]
    out_ref[...] = out_in[...]
    width = qkv_ref.shape[2]
    for n in range(3):
        qkv_ref[n] = qkv_in[:, n * width : (n + 1) * width]
    qv_ref[...] = late_in[2:4, :]
    first_gain, first_shift, out_bias, gain, shift, fc_bias, proj_bias = vectors
    lanes = first_gain.shape[1]
    count = first_gain.shape[0]
    singles = ((first_gain, late_in, 0), (first_shift, late_in, 1), (out_bias, early_in, 0))
    singles += ((gain, early_in, 1), (shift, early_in, 2), (proj_bias, early_in, 3))
    for ref, source, row in singles:
        for n in range(count):
            ref[n : n + 1, :] = source[row : row + 1, n * lanes : (n + 1) * lanes]
    for row in range(4):
        for n in range(count):
            at = row * count + n
            fc_bias[at : at + 1, :] = early_in[4 + row : 5 + row, n * lanes : (n + 1) * lanes]


def finish(rows, fc, proj, out, qkv, early, late):
    lanes = 128
    width = late.shape[1]
    shapes = [rows, fc, proj, out]
    outs = [jax.ShapeDtypeStruct(v.shape, v.dtype) for v in shapes]
    outs.append(jax.ShapeDtypeStruct((3, qkv.shape[0], qkv.shape[1] // 3), f32))
    outs.append(jax.ShapeDtypeStruct((2, width), f32))
    sizes = [width] * 5 + [4 * early.shape[1], width]
    outs += [jax.ShapeDtypeStruct((n // lanes, lanes), f32) for n in sizes]
    rows, fc, proj, out, qkv, qv, *vectors = pl.pallas_call(
        finish_kernel,
        out_shape=outs,
        in_specs=[in_vmem()] * 7,
        out_specs=[in_vmem()] * len(outs),
        cost_estimate=pl.CostEstimate(flops=0, bytes_accessed=3 << 20, transcendentals=0),
        name="finish",
    )(rows, fc, proj, out, qkv, early, late)
    return rows, fc, proj.T, out.T, qkv.transpose(1, 0, 2), qv, [v.reshape(-1) for v in vectors]


def flip(axis, bit):
    me = lax.axis_index(axis)
    return me + bit - 2 * bit * lax.rem(me // bit, 2)


def bits_of(axis):
    size, bits, bit = lax.axis_size(axis), [], 1
    while bit < size:
        bits.append((axis, bit))
        bit *= 2
    return bits


def across(value):
    return lax.ppermute(value, "tp", [(n, n ^ 2) for n in range(4)])


def local(
    inputs,
    segments,
    out_grad,
    first_gain,
    first_shift,
    qkv_weight,
    qv_bias,
    out_weight,
    out_bias,
    second_gain,
    second_shift,
    fc_weight,
    fc_bias,
    proj_weight,
    proj_bias,
):
    slices = lax.axis_size("tp")
    rows_here, model_width = inputs.shape
    shard_rows = qkv_weight.shape[0]
    head_cols = qkv_weight.shape[2]
    hidden_cols = fc_weight.shape[1]
    params = jnp.concatenate(
        [
            jnp.stack([out_bias, second_gain, second_shift, proj_bias]),
            fc_bias.reshape(slices, hidden_cols),
            jnp.stack([first_gain, first_shift]),
            qv_bias,
            jnp.zeros((4, model_width), bf16),
        ]
    ).astype(f32)
    size = min(BLOCK, rows_here)
    seq_normed, seg_parts, low, qa, ka, va, vt, kt, qkv_full, own = enter(
        inputs,
        params,
        segments,
        (qkv_weight.reshape(shard_rows, 3 * head_cols), fc_weight, proj_weight.T, out_weight.T),
        size,
        0,
    )
    qkv_full = qkv_full.reshape(model_width, 3 * head_cols)
    own = own.reshape(model_width, own.shape[2])
    over = across(own)
    widths = (hidden_cols, hidden_cols, head_cols)

    attn_out, qb = attend(low, qa, ka, vt, seg_parts, size)

    layer_out, grad_hidden, grad_attn_seq, kept, passed, early = middle(
        attn_out, own, over, inputs, out_grad, segments, params, hidden_cols, 2
    )
    came = across(passed)
    grad_qkv = attend_back(low, qb, ka, va, kt, grad_attn_seq, attn_out, seg_parts, size)
    input_grad, fc_w_grad, proj_w_grad, out_w_grad, qkv_grad, early_sums, late_sums = leave(
        grad_qkv,
        seq_normed,
        qkv_full,
        kept,
        came,
        widths,
        early,
        inputs,
        params,
        grad_hidden,
        3,
    )
    input_grad, fc_w_grad, proj_w_grad, out_w_grad, qkv_grad, qv_bias_grad, vectors = finish(
        input_grad,
        fc_w_grad,
        proj_w_grad,
        out_w_grad,
        qkv_grad,
        early_sums,
        late_sums,
    )
    first_gain_grad, first_shift_grad, out_bias_grad, second_gain_grad, second_shift_grad = vectors[0:5]
    fc_bias_grad, proj_bias_grad = vectors[5:7]

    return (
        layer_out,
        input_grad,
        first_gain_grad,
        first_shift_grad,
        qkv_grad,
        qv_bias_grad,
        out_w_grad,
        out_bias_grad,
        second_gain_grad,
        second_shift_grad,
        fc_w_grad,
        fc_bias_grad,
        proj_w_grad,
        proj_bias_grad,
    )


def solution(mesh):
    return jax.shard_map(
        local,
        mesh=mesh,
        in_specs=(
            P(("fsdp", "tp"), None),
            P("fsdp", "tp"),
            P(("fsdp", "tp"), None),
            P(),
            P(),
            P("fsdp", None, "tp"),
            P(),
            P("tp", "fsdp"),
            P(),
            P(),
            P(),
            P("fsdp", "tp"),
            P(),
            P("tp", "fsdp"),
            P(),
        ),
        out_specs=(
            P(("fsdp", "tp"), None),
            P(("fsdp", "tp"), None),
            P(),
            P(),
            P("fsdp", None, "tp"),
            P(),
            P("tp", "fsdp"),
            P(),
            P(),
            P(),
            P("fsdp", "tp"),
            P(),
            P("tp", "fsdp"),
            P(),
        ),
        check_vma=False,
    )
```

profile of v0, /device:TPU:0, one launch (start us, length us, event | category | flops | bytes accessed | tf_op | source)
XLA Modules:
  0.0 208.6 jit_solution(9612375486408419717)
XLA Ops:
  0.6 0.0 copy-start
  0.7 0.7 stack.22
  1.4 0.7 stack.23
  2.0 0.7 stack.18
  2.7 0.7 stack.19
  3.4 0.7 stack.20
  4.1 0.7 stack.21
  4.8 0.7 reshape.67
  5.5 0.7 concatenate.3
  6.2 0.6 convert_element_type.3.par_ref.gain_ref
  6.8 0.6 copy_bitcast_fusion.w0
  7.5 42.3 %enter.1 = (bf16[4096,512]{1,0:T(8,128)(2,1)}, s32[4,1,1024]{2,1,0:T(1,128)}, s32[8,128]{1,0:T(8,128)}, bf16[2,4096,128]{2,1,0:T(8,128)(2,1)}, bf16[2,4096,128]{...) custom-call(bf16[1024,512]{1,0:T(8,128)(2,1)} %x_in.1, ...), custom_call_target="tpu_custom_call" | custom-call | bytes 62914560 | tf_op jit(solution)/shard_map/enter/pallas_call | solution.py:272
  49.7 1.2 collective-permute-start
  51.0 23.7 %attend.1 = (bf16[4096,128]{1,0:T(8,128)(2,1)}, bf16[2,4096,128]{2,1,0:T(8,128)(2,1)}) custom-call(s32[8,128]{1,0:T(8,128)} %get-tuple-element.52.low_ref, bf16[2,4096,128]{2,1,0:T(8,128)(2,1)} %get-tuple-element.53.qa_ref, bf16[2,4096,128]{2,1,0:T(8,128)(2,1)} %get-tuple-element.54.ka_ref, bf16[2,80,4096]{2,1,0:T(8,128)(2,1)} %get-tuple-element.55.vt_ref, ...), custom_call_target="tpu_custom_call" | custom-call | flops 30064771072 | bytes 8388608 | tf_op jit(solution)/shard_map/attend/pallas_call | solution.py:126
  74.7 1.6 collective-permute-done.passed_ref
  76.3 1.0 copy-done.2
  77.3 41.0 %middle.1 = (bf16[1024,512]{1,0:T(8,128)(2,1)}, f32[1024,512]{1,0:T(8,128)}, bf16[4096,128]{1,0:T(8,128)(2,1)}, bf16[512,1152]{1,0:T(8,128)(2,1)}, bf16[512,1152]{1,0:T(8,128)(2,1)}, /*index=5*/f32[8,512]{1,0:T(8,128)}) custom-call(bf16[4096,128]{1,0:T(8,128)(2,1)} %get-tuple-element.57.seq_out.o_ref, bf16[512,1152]{1,0:T(8,128)(2,1)} %bitcast.24, ...), custom_call_target="tpu_custom_call" | custom-call | bytes 62914560 | tf_op jit(solution)/shard_map/middle/pallas_call | solution.py:272
  118.3 0.8 collective-permute-start.1
  119.1 31.3 %attend_back.1.grad_ref = bf16[4096,384]{1,0:T(8,128)(2,1)} custom-call(s32[8,128]{1,0:T(8,128)} %get-tuple-element.52.low_ref, bf16[2,4096,128]{2,1,0:T(8,128)(2,1)} %get-tuple-element.60.qb_ref, bf16[2,4096,128]{2,1,0:T(8,128)(2,1)} %get-tuple-element.54.ka_ref, bf16[2,4096,128]{2,1,0:T(8,128)(2,1)} %get-tuple-element.61.va_ref, ...), custom_call_target="tpu_custom_call" | custom-call | flops 51539607552 | bytes 16777216 | tf_op jit(solution)/shard_map/attend_back/pallas_call | solution.py:217
  150.4 0.0 collective-permute-done.1
  150.4 1.1 copy-done.1
  151.5 53.5 %leave.1 = (bf16[1024,512]{1,0:T(8,128)(2,1)}, f32[64,512]{1,0:T(8,128)}, f32[64,512]{1,0:T(8,128)}, f32[64,128]{1,0:T(8,128)}, f32[64,384]{1,0:T(8,128)}, /*index=5*/f32[8,512]{1,0:T(8,128)}, f32[4,512]{1,0:T(4,128)}) custom-call(bf16[4096,384]{1,0:T(8,128)(2,1)} %attend_back.1.grad_ref, bf16[4096,512]{1,0:T(8,128)(2,1)} %get-tuple-element.64.normed_in, ...), custom_call_target="tpu_custom_call" | custom-call | bytes 62914560 | tf_op jit(solution)/shard_map/leave/pallas_call | solution.py:272
  205.0 2.6 %finish.1 = (bf16[1024,512]{1,0:T(8,128)(2,1)}, f32[64,512]{1,0:T(8,128)}, f32[64,512]{1,0:T(8,128)}, f32[64,128]{1,0:T(8,128)}, f32[3,64,128]{2,1,0:T(8,128)}, ...) custom-call(bf16[1024,512]{1,0:T(8,128)(2,1)} %get-tuple-element.70., ...), custom_call_target="tpu_custom_call" | custom-call | bytes 3145728 | tf_op jit(solution)/shard_map/finish/pallas_call | solution.py:1051
  207.6 1.0 copy.34
  (6 shorter events, 0.0 us)
Async XLA Ops:
  0.6 6.2 %copy-start = (bf16[64,3,128]{2,0,1:T(8,128)(2,1)S(1)}, bf16[64,3,128]{2,0,1:T(8,128)(2,1)}, u32[]{:S(2)}) copy-start(bf16[64,3,128]{2,0,1:T(8,128)(2,1)} %param.20) | copy-start | bytes 147460
  49.7 26.5 %collective-permute-start = (bf16[512,1152]{1,0:T(8,128)(2,1)}, bf16[512,1152]{1,0:T(8,128)(2,1)S(1)}, u32[]{:S(2)}, u32[]{:S(2)}) collective-permute-start(bf16[512,1152]{1,0:T(8,128)(2,1)} %bitcast.23), channel_id=1, source_target_pairs={{0,2},{1,3},{2,0},{3,1},{4,6},{5,7},{6,4},{7,5},{8,10},{9,11},{10,... | collective-permute-start | bytes 3538952 | tf_op jit(solution)/shard_map/ppermute | solution.py:1076
  76.3 1.0 copy-start.2
  118.3 32.1 %collective-permute-start.1 = (bf16[512,1152]{1,0:T(8,128)(2,1)}, bf16[512,1152]{1,0:T(8,128)(2,1)S(1)}, u32[]{:S(2)}, u32[]{:S(2)}) collective-permute-start(bf16[512,1152]{1,0:T(8,128)(2,1)} %get-tuple-element.67), channel_id=1, source_target_pairs={{0,2},{1,3},{2,0},{3,1},{4,6},{5,7},{6,4},{7,5},{8,10},{9,11},{10,... | collective-permute-start | bytes 3538952 | tf_op jit(solution)/shard_map/ppermute | solution.py:1076
  150.4 1.1 copy-start.1
  205.0 2.6 %copy-start.3 = (bf16[1024,512]{1,0:T(8,128)(2,1)S(1)}, bf16[1024,512]{1,0:T(8,128)(2,1)}, u32[]{:S(2)}) copy-start(bf16[1024,512]{1,0:T(8,128)(2,1)} %get-tuple-element.104) | copy-start | bytes 3145732
where the time goes:
time: 213 us; the launch traced here: 209 us
  Pallas kernels  194 us (91%)
  local copies, waits for them, and re-layouts  9.24 us (4%)
    pallas_call x3, Pallas kernels, comm_call(): pl.pallas_call(kernel, out_shape=out_shape, in_specs=in_specs, out_specs=...  137 us
    pallas_call x1, Pallas kernels, attend_back(): pl.pallas_call(functools.partial(attend_back_kernel, size=size, blocks=ro...  31.3 us
    pallas_call x1, Pallas kernels, attend(): pl.pallas_call(functools.partial(attend_kernel, size=size, blocks=rows //...  23.7 us
  transfers between devices with their start and end apart: 2, of which 1 were waited for; matrix products, arithmetic and copies ran while one was open for 0% of the time, Pallas kernels for 26%

commit v1 on v0

--- a/solution.py
+++ b/solution.py
@@ -313,8 +313,8 @@
 
 
 def enter_kernel(
-    x_ref, par_ref, seg_ref, w0, w1, w2, w3,
-    normed_ref, segs_ref, low_ref, qa_ref, ka_ref, va_ref, vt_ref, kt_ref, f0, f1,
+    x_ref, seg_ref, w0, w1, w2, w3, v0, v1, v2, v3, v4, v5, v6, v7,
+    normed_ref, segs_ref, low_ref, par_ref, qa_ref, ka_ref, va_ref, vt_ref, kt_ref, f0, f1,
     x_all, normed_s, qa_s, ka_s, va_s, vt_s, kt_s,
     sy, ry, ss, rs, sf, rf, sg, rg, sw, rw, own, own_w, outs, *, parts, size
 ):
@@ -391,6 +391,15 @@
         awaited(rows_of(side, part), ss.at[part], rs.at[part], {"tp": side}).wait_recv()
     for copy in kept:
         copy.wait()
+
+    line, columns = 0, par_ref.shape[1]
+    par_ref[...] = jnp.zeros_like(par_ref)
+    for ref in (v0, v1, v2, v3, v4, v5, v6):
+        value = ref[...].astype(f32).reshape(1, ref.shape[0])
+        for n in range(ref.shape[0] // columns):
+            par_ref[line : line + 1, :] = value[:, n * columns : (n + 1) * columns]
+            line += 1
+    par_ref[line : line + 2, :] = v7[...].astype(f32)
     gain, shift = par_ref[8:9, :], par_ref[9:10, :]
 
     def norm(owner, part):
@@ -502,7 +511,7 @@
         copy.wait_send()
 
 
-def enter(x, params, segments, weights, size, number, parts=4):
+def enter(x, vectors, segments, weights, size, number, parts=2):
     rows, width = x.shape
     seq_rows = 4 * rows
     shards = lax.axis_size("fsdp")
@@ -518,11 +527,11 @@
         "enter",
         number,
         [made[0], jax.ShapeDtypeStruct((4, *segments.shape), segments.dtype)]
-        + [jax.ShapeDtypeStruct((seq_rows // size, 128), jnp.int32)]
+        + [jax.ShapeDtypeStruct((seq_rows // size, 128), jnp.int32), jax.ShapeDtypeStruct((16, width), f32)]
         + made[1:]
         + [jax.ShapeDtypeStruct(s, bf16) for s in full],
-        [in_vmem()] * 7,
-        [anywhere(), in_vmem(), in_vmem()] + [anywhere()] * 5 + [in_vmem(), anywhere()],
+        [in_vmem()] * (6 + len(vectors)),
+        [anywhere()] + [in_vmem()] * 3 + [anywhere()] * 5 + [in_vmem(), anywhere()],
         [pltpu.VMEM((seq_rows, width), bf16)]
         + [pltpu.VMEM(s, bf16) for s in shapes]
         + [dma((parts,))] * 6
@@ -531,9 +540,9 @@
         + [dma((2,)), dma((4,)), dma((6, 4 * parts))],
         60 << 20,
         x,
-        params,
         segments,
         *weights,
+        *vectors,
     )
 
 
@@ -646,7 +655,7 @@
 
     lax.fori_loop(0, parts, row_block, 0)
     width = out_acc.shape[1]
-    tall = 128
+    tall = 256
 
     def out_block(n, carry):
         at = pl.ds(pl.multiple_of(n * tall, tall), tall)
@@ -708,7 +717,7 @@
             awaited(grad.at[2 * b + 1], ws.at[n, b], wr.at[n, b], {"tp": side}).wait_send()
 
 
-def middle(attn, own, passed, x, grad, segments, params, hidden, number, parts=4):
+def middle(attn, own, passed, x, grad, segments, params, hidden, number, parts=2):
     rows, lanes = x.shape[0], attn.shape[1]
     width = x.shape[1]
     fc = pj = (4, width, hidden)
@@ -964,7 +973,7 @@
         copy.wait_send()
 
 
-def leave(grad, normed, w, kept, came, widths, early, x, gain, resid, number, parts=4):
+def leave(grad, normed, w, kept, came, widths, early, x, gain, resid, number, parts=2):
     rows, width = grad.shape[0] // 4, w.shape[0]
     dma = pltpu.SemaphoreType.DMA
     hops = bits_of("fsdp")
@@ -1098,19 +1107,11 @@
     shard_rows = qkv_weight.shape[0]
     head_cols = qkv_weight.shape[2]
     hidden_cols = fc_weight.shape[1]
-    params = jnp.concatenate(
-        [
-            jnp.stack([out_bias, second_gain, second_shift, proj_bias]),
-            fc_bias.reshape(slices, hidden_cols),
-            jnp.stack([first_gain, first_shift]),
-            qv_bias,
-            jnp.zeros((4, model_width), bf16),
-        ]
-    ).astype(f32)
+    vectors = (out_bias, second_gain, second_shift, proj_bias, fc_bias, first_gain, first_shift, qv_bias)
     size = min(BLOCK, rows_here)
-    seq_normed, seg_parts, low, qa, ka, va, vt, kt, qkv_full, own = enter(
+    seq_normed, seg_parts, low, params, qa, ka, va, vt, kt, qkv_full, own = enter(
         inputs,
-        params,
+        vectors,
         segments,
         (qkv_weight.reshape(shard_rows, 3 * head_cols), fc_weight, proj_weight.T, out_weight.T),
         size,

time: 213 us -> 201 us (0.944); the launches traced: 209 us -> 201 us
  local copies, waits for them, and re-layouts: 9.24 us -> 4.51 us
  Pallas kernels: 194 us -> 191 us
    another operation x6 -> x0, local copies, waits for them, and re-layouts: 4.1 us -> none  [the longest x4 2.73 us: local(): jnp.stack([out_bias, second_gain, second_shift, proj_bias])]
where the time goes in v1:
time: 201 us
  Pallas kernels  191 us (95%)
  local copies, waits for them, and re-layouts  4.51 us (2%)
  waiting for transfers between devices  3.53 us (2%)
    pallas_call x3, Pallas kernels, comm_call(): pl.pallas_call(kernel, out_shape=out_shape, in_specs=in_specs, out_specs=...  135 us
    pallas_call x1, Pallas kernels, attend_back(): pl.pallas_call(functools.partial(attend_back_kernel, size=size, blocks=ro...  30 us
    pallas_call x1, Pallas kernels, attend(): pl.pallas_call(functools.partial(attend_kernel, size=size, blocks=rows //...  23 us
  transfers between devices with their start and end apart: 2, of which 1 were waited for; matrix products, arithmetic and copies ran while one was open for 0% of the time, Pallas kernels for 26%

profile of v1, /device:TPU:0, one launch (start us, length us, event | category | flops | bytes accessed | tf_op | source)
XLA Modules:
  0.0 201.1 jit_solution(13327009780974804601)
XLA Ops:
  0.6 0.0 copy-start
  0.7 0.8 copy-done
  1.4 0.6 copy_bitcast_fusion.w0
  2.1 38.7 %enter.1 = (bf16[4096,512]{1,0:T(8,128)(2,1)}, s32[4,1,1024]{2,1,0:T(1,128)}, s32[8,128]{1,0:T(8,128)}, f32[16,512]{1,0:T(8,128)}, bf16[2,4096,128]{2,1,0:T(8,12...) custom-call(bf16[1024,512]{1,0:T(8,128)(2,1)} %x_in.1, ...), custom_call_target="tpu_custom_call" | custom-call | bytes 62914560 | tf_op jit(solution)/shard_map/enter/pallas_call | solution.py:272
  40.8 0.7 collective-permute-start
  41.5 23.0 %attend.1 = (bf16[4096,128]{1,0:T(8,128)(2,1)}, bf16[2,4096,128]{2,1,0:T(8,128)(2,1)}) custom-call(s32[8,128]{1,0:T(8,128)} %get-tuple-element.53.low_ref, bf16[2,4096,128]{2,1,0:T(8,128)(2,1)} %get-tuple-element.54.qa_ref, bf16[2,4096,128]{2,1,0:T(8,128)(2,1)} %get-tuple-element.55.ka_ref, bf16[2,80,4096]{2,1,0:T(8,128)(2,1)} %get-tuple-element.56.vt_ref, ...), custom_call_target="tpu_custom_call" | custom-call | flops 30064771072 | bytes 8388608 | tf_op jit(solution)/shard_map/attend/pallas_call | solution.py:126
  64.4 3.5 %collective-permute-done.passed_ref = bf16[512,1152]{1,0:T(8,128)(2,1)S(1)} collective-permute-done((bf16[512,1152]{1,0:T(8,128)(2,1)}, bf16[512,1152]{1,0:T(8,128)(2,1)S(1)}, u32[]{:S(2)}, u32[]{:S(2)}) %collective-permute-start) | collective-permute-done | bytes 1179680 | tf_op jit(solution)/shard_map/ppermute | solution.py:1085
  68.0 0.0 copy-start.2
  68.0 1.0 copy-done.2
  69.0 37.2 %middle.1 = (bf16[1024,512]{1,0:T(8,128)(2,1)}, f32[1024,512]{1,0:T(8,128)}, bf16[4096,128]{1,0:T(8,128)(2,1)}, bf16[512,1152]{1,0:T(8,128)(2,1)}, bf16[512,1152]{1,0:T(8,128)(2,1)}, /*index=5*/f32[8,512]{1,0:T(8,128)}) custom-call(bf16[4096,128]{1,0:T(8,128)(2,1)} %get-tuple-element.58.seq_out.o_ref, bf16[512,1152]{1,0:T(8,128)(2,1)} %bitcast.24, ...), custom_call_target="tpu_custom_call" | custom-call | bytes 62914560 | tf_op jit(solution)/shard_map/middle/pallas_call | solution.py:272
  106.2 0.7 collective-permute-start.1
  106.9 30.0 %attend_back.1.grad_ref = bf16[4096,384]{1,0:T(8,128)(2,1)} custom-call(s32[8,128]{1,0:T(8,128)} %get-tuple-element.53.low_ref, bf16[2,4096,128]{2,1,0:T(8,128)(2,1)} %get-tuple-element.62.qb_ref, bf16[2,4096,128]{2,1,0:T(8,128)(2,1)} %get-tuple-element.55.ka_ref, bf16[2,4096,128]{2,1,0:T(8,128)(2,1)} %get-tuple-element.63.va_ref, ...), custom_call_target="tpu_custom_call" | custom-call | flops 51539607552 | bytes 16777216 | tf_op jit(solution)/shard_map/attend_back/pallas_call | solution.py:217
  136.9 0.0 collective-permute-done.1
  136.9 0.0 copy-start.1
  136.9 1.1 copy-done.1
  138.0 59.5 %leave.1 = (bf16[1024,512]{1,0:T(8,128)(2,1)}, f32[64,512]{1,0:T(8,128)}, f32[64,512]{1,0:T(8,128)}, f32[64,128]{1,0:T(8,128)}, f32[64,384]{1,0:T(8,128)}, /*index=5*/f32[8,512]{1,0:T(8,128)}, f32[4,512]{1,0:T(4,128)}) custom-call(bf16[4096,384]{1,0:T(8,128)(2,1)} %attend_back.1.grad_ref, bf16[4096,512]{1,0:T(8,128)(2,1)} %get-tuple-element.66.normed_in, ...), custom_call_target="tpu_custom_call" | custom-call | bytes 62914560 | tf_op jit(solution)/shard_map/leave/pallas_call | solution.py:272
  197.5 0.0 copy-start.3
  197.5 2.6 %finish.1 = (bf16[1024,512]{1,0:T(8,128)(2,1)}, f32[64,512]{1,0:T(8,128)}, f32[64,512]{1,0:T(8,128)}, f32[64,128]{1,0:T(8,128)}, f32[3,64,128]{2,1,0:T(8,128)}, ...) custom-call(bf16[1024,512]{1,0:T(8,128)(2,1)} %get-tuple-element.72., ...), custom_call_target="tpu_custom_call" | custom-call | bytes 3145728 | tf_op jit(solution)/shard_map/finish/pallas_call | solution.py:1060
  200.1 0.0 copy-done.3
  200.1 1.0 copy.34
Async XLA Ops:
  0.6 0.8 copy-start
  40.8 27.2 %collective-permute-start = (bf16[512,1152]{1,0:T(8,128)(2,1)}, bf16[512,1152]{1,0:T(8,128)(2,1)S(1)}, u32[]{:S(2)}, u32[]{:S(2)}) collective-permute-start(bf16[512,1152]{1,0:T(8,128)(2,1)} %bitcast.23), channel_id=1, source_target_pairs={{0,2},{1,3},{2,0},{3,1},{4,6},{5,7},{6,4},{7,5},{8,10},{9,11},{10,... | collective-permute-start | bytes 3538952 | tf_op jit(solution)/shard_map/ppermute | solution.py:1085
  68.0 1.0 copy-start.2
  106.2 30.7 %collective-permute-start.1 = (bf16[512,1152]{1,0:T(8,128)(2,1)}, bf16[512,1152]{1,0:T(8,128)(2,1)S(1)}, u32[]{:S(2)}, u32[]{:S(2)}) collective-permute-start(bf16[512,1152]{1,0:T(8,128)(2,1)} %get-tuple-element.69), channel_id=1, source_target_pairs={{0,2},{1,3},{2,0},{3,1},{4,6},{5,7},{6,4},{7,5},{8,10},{9,11},{10,... | collective-permute-start | bytes 3538952 | tf_op jit(solution)/shard_map/ppermute | solution.py:1085
  136.9 1.1 copy-start.1
  197.5 2.6 %copy-start.3 = (bf16[1024,512]{1,0:T(8,128)(2,1)S(1)}, bf16[1024,512]{1,0:T(8,128)(2,1)}, u32[]{:S(2)}) copy-start(bf16[1024,512]{1,0:T(8,128)(2,1)} %get-tuple-element.106) | copy-start | bytes 3145732

commit v2 on v1

--- a/solution.py
+++ b/solution.py
@@ -655,7 +655,7 @@
 
     lax.fori_loop(0, parts, row_block, 0)
     width = out_acc.shape[1]
-    tall = 256
+    tall = 512
 
     def out_block(n, carry):
         at = pl.ds(pl.multiple_of(n * tall, tall), tall)
@@ -791,6 +791,7 @@
     pl.semaphore_wait(barrier, 3 + shards - 1)
     count = len(hops)
     outs = (s0, s1, s2, s3)
+    swapped = (0, 2) if count > 1 else ()
     current = bufs[0:4]
     boxes = [bufs[4 + g * count : 4 + (g + 1) * count] for g in range(4)]
     keeps = [bufs[4 + 4 * count + g * (count - 1) : 4 + 4 * count + (g + 1) * (count - 1)] for g in range(4)]
@@ -799,11 +800,18 @@
     def begin(g):
         at = sum(c.shape[3] for c in current[0:g])
         cols = slice(at, at + current[g].shape[3])
-        total = kept_ref[:, :, :, cols].astype(f32) + came_ref[:, :, :, cols].astype(f32)
-        current[g][...] = total.astype(bf16)
+        if g not in swapped:
+            total = kept_ref[:, :, :, cols].astype(f32) + came_ref[:, :, :, cols].astype(f32)
+            current[g][...] = total.astype(bf16)
+            return
+        for p in range(current[g].shape[0]):
+            for q in range(2):
+                i, j = (p // 2) * 2 + q, p % 2
+                total = kept_ref[i, j, :, cols].astype(f32) + came_ref[i, j, :, cols].astype(f32)
+                current[g][p, q] = total.astype(bf16)
 
     def hop_parts(g, k):
-        axis, bit = hops[k]
+        axis, bit = hops[(1, 0, *range(2, count))[k] if g in swapped else k]
         source = current[g] if k == 0 else keeps[g][k - 1]
         half = lax.rem(lax.axis_index(axis) // bit, 2)
         return {axis: flip(axis, bit)}, source, half, boxes[g][k]
@@ -929,10 +937,11 @@
         return carry
 
     tp_send(early_ref, early_one, se, re)
+    begin(0)
+    hop_send(0, 0)
     lax.fori_loop(0, parts, give_far, 0)
-    for g in (0, 1):
-        begin(g)
-        hop_send(g, 0)
+    begin(1)
+    hop_send(1, 0)
     lax.fori_loop(0, parts, give_over, 0)
     begin(2)
     for copy in loading:

time: 201 us -> 196 us (0.975); the launches traced: 201 us -> 199 us
  waiting for transfers between devices: 3.53 us -> 0.01 us
    pallas_call x3, Pallas kernels: 135 us -> 126 us  [comm_call(): pl.pallas_call(kernel, out_shape=out_shape, in_specs=in_specs, out_specs=...]
    pallas_call x1, Pallas kernels: 30 us -> 37.1 us  [attend_back(): pl.pallas_call(functools.partial(attend_back_kernel, size=size, blocks=ro...]
    pallas_call x1, Pallas kernels: 23 us -> 26.6 us  [attend(): pl.pallas_call(functools.partial(attend_kernel, size=size, blocks=rows //...]
    ppermute x2, waiting for transfers between devices: 3.53 us -> 0.01 us  [across(): return lax.ppermute(value, 'tp', [(n, n ^ 2) for n in range(4)])]
  transfers between devices with their start and end apart: 2 -> 2, of which waited for: 1 -> 0; matrix products, arithmetic and copies ran while one was open for 0% -> 0% of each run, Pallas kernels for 26% -> 32%
where the time goes in v2:
time: 196 us; the launch traced here: 199 us
  Pallas kernels  192 us (98%)
  local copies, waits for them, and re-layouts  4.51 us (2%)
    pallas_call x3, Pallas kernels, comm_call(): pl.pallas_call(kernel, out_shape=out_shape, in_specs=in_specs, out_specs=...  126 us
    pallas_call x1, Pallas kernels, attend_back(): pl.pallas_call(functools.partial(attend_back_kernel, size=size, blocks=ro...  37.1 us
    pallas_call x1, Pallas kernels, attend(): pl.pallas_call(functools.partial(attend_kernel, size=size, blocks=rows //...  26.6 us
  transfers between devices with their start and end apart: 2, of which 0 were waited for; matrix products, arithmetic and copies ran while one was open for 0% of the time, Pallas kernels for 32%

profile of v2, /device:TPU:0, one launch (start us, length us, event | category | flops | bytes accessed | tf_op | source)
XLA Modules:
  0.0 199.0 jit_solution(17821824139054767702)
XLA Ops:
  0.6 0.0 copy-start
  0.7 0.8 copy-done
  1.4 0.6 copy_bitcast_fusion.w0
  2.1 38.7 %enter.1 = (bf16[4096,512]{1,0:T(8,128)(2,1)}, s32[4,1,1024]{2,1,0:T(1,128)}, s32[8,128]{1,0:T(8,128)}, f32[16,512]{1,0:T(8,128)}, bf16[2,4096,128]{2,1,0:T(8,12...) custom-call(bf16[1024,512]{1,0:T(8,128)(2,1)} %x_in.1, ...), custom_call_target="tpu_custom_call" | custom-call | bytes 62914560 | tf_op jit(solution)/shard_map/enter/pallas_call | solution.py:272
  40.8 0.7 collective-permute-start
  41.5 26.6 %attend.1 = (bf16[4096,128]{1,0:T(8,128)(2,1)}, bf16[2,4096,128]{2,1,0:T(8,128)(2,1)}) custom-call(s32[8,128]{1,0:T(8,128)} %get-tuple-element.53.low_ref, bf16[2,4096,128]{2,1,0:T(8,128)(2,1)} %get-tuple-element.54.qa_ref, bf16[2,4096,128]{2,1,0:T(8,128)(2,1)} %get-tuple-element.55.ka_ref, bf16[2,80,4096]{2,1,0:T(8,128)(2,1)} %get-tuple-element.56.vt_ref, ...), custom_call_target="tpu_custom_call" | custom-call | flops 30064771072 | bytes 8388608 | tf_op jit(solution)/shard_map/attend/pallas_call | solution.py:126
  68.1 0.0 collective-permute-done.passed_ref
  68.1 0.0 copy-start.2
  68.1 1.0 copy-done.2
  69.1 36.8 %middle.1 = (bf16[1024,512]{1,0:T(8,128)(2,1)}, f32[1024,512]{1,0:T(8,128)}, bf16[4096,128]{1,0:T(8,128)(2,1)}, bf16[512,1152]{1,0:T(8,128)(2,1)}, bf16[512,1152]{1,0:T(8,128)(2,1)}, /*index=5*/f32[8,512]{1,0:T(8,128)}) custom-call(bf16[4096,128]{1,0:T(8,128)(2,1)} %get-tuple-element.58.seq_out.o_ref, bf16[512,1152]{1,0:T(8,128)(2,1)} %bitcast.24, ...), custom_call_target="tpu_custom_call" | custom-call | bytes 62914560 | tf_op jit(solution)/shard_map/middle/pallas_call | solution.py:272
  106.0 1.0 collective-permute-start.1
  107.0 37.1 %attend_back.1.grad_ref = bf16[4096,384]{1,0:T(8,128)(2,1)} custom-call(s32[8,128]{1,0:T(8,128)} %get-tuple-element.53.low_ref, bf16[2,4096,128]{2,1,0:T(8,128)(2,1)} %get-tuple-element.62.qb_ref, bf16[2,4096,128]{2,1,0:T(8,128)(2,1)} %get-tuple-element.55.ka_ref, bf16[2,4096,128]{2,1,0:T(8,128)(2,1)} %get-tuple-element.63.va_ref, ...), custom_call_target="tpu_custom_call" | custom-call | flops 51539607552 | bytes 16777216 | tf_op jit(solution)/shard_map/attend_back/pallas_call | solution.py:217
  144.1 0.0 collective-permute-done.1
  144.1 0.0 copy-start.1
  144.1 1.1 copy-done.1
  145.2 50.2 %leave.1 = (bf16[1024,512]{1,0:T(8,128)(2,1)}, f32[64,512]{1,0:T(8,128)}, f32[64,512]{1,0:T(8,128)}, f32[64,128]{1,0:T(8,128)}, f32[64,384]{1,0:T(8,128)}, /*index=5*/f32[8,512]{1,0:T(8,128)}, f32[4,512]{1,0:T(4,128)}) custom-call(bf16[4096,384]{1,0:T(8,128)(2,1)} %attend_back.1.grad_ref, bf16[4096,512]{1,0:T(8,128)(2,1)} %get-tuple-element.66.normed_in, ...), custom_call_target="tpu_custom_call" | custom-call | bytes 62914560 | tf_op jit(solution)/shard_map/leave/pallas_call | solution.py:272
  195.4 0.0 copy-start.3
  195.4 2.6 %finish.1 = (bf16[1024,512]{1,0:T(8,128)(2,1)}, f32[64,512]{1,0:T(8,128)}, f32[64,512]{1,0:T(8,128)}, f32[64,128]{1,0:T(8,128)}, f32[3,64,128]{2,1,0:T(8,128)}, ...) custom-call(bf16[1024,512]{1,0:T(8,128)(2,1)} %get-tuple-element.72., ...), custom_call_target="tpu_custom_call" | custom-call | bytes 3145728 | tf_op jit(solution)/shard_map/finish/pallas_call | solution.py:1069
  198.0 0.0 copy-done.3
  198.0 1.0 copy.34
Async XLA Ops:
  0.6 0.8 copy-start
  40.8 27.3 %collective-permute-start = (bf16[512,1152]{1,0:T(8,128)(2,1)}, bf16[512,1152]{1,0:T(8,128)(2,1)S(1)}, u32[]{:S(2)}, u32[]{:S(2)}) collective-permute-start(bf16[512,1152]{1,0:T(8,128)(2,1)} %bitcast.23), channel_id=1, source_target_pairs={{0,2},{1,3},{2,0},{3,1},{4,6},{5,7},{6,4},{7,5},{8,10},{9,11},{10,... | collective-permute-start | bytes 3538952 | tf_op jit(solution)/shard_map/ppermute | solution.py:1094
  68.1 1.0 copy-start.2
  106.0 38.1 %collective-permute-start.1 = (bf16[512,1152]{1,0:T(8,128)(2,1)}, bf16[512,1152]{1,0:T(8,128)(2,1)S(1)}, u32[]{:S(2)}, u32[]{:S(2)}) collective-permute-start(bf16[512,1152]{1,0:T(8,128)(2,1)} %get-tuple-element.69), channel_id=1, source_target_pairs={{0,2},{1,3},{2,0},{3,1},{4,6},{5,7},{6,4},{7,5},{8,10},{9,11},{10,... | collective-permute-start | bytes 3538952 | tf_op jit(solution)/shard_map/ppermute | solution.py:1094
  144.1 1.1 copy-start.1
  195.4 2.6 %copy-start.3 = (bf16[1024,512]{1,0:T(8,128)(2,1)S(1)}, bf16[1024,512]{1,0:T(8,128)(2,1)}, u32[]{:S(2)}) copy-start(bf16[1024,512]{1,0:T(8,128)(2,1)} %get-tuple-element.106) | copy-start | bytes 3145732

commit v3 on v2

--- a/solution.py
+++ b/solution.py
@@ -921,7 +921,7 @@
         awaited(sum_buf.at[here], sy.at[part], ry.at[part], {"tp": across}).wait_send()
         return carry
 
-    chunk = 512
+    chunk = 1024
     steps = grad_ref.shape[0] // chunk
     dw_acc[...] = jnp.zeros_like(dw_acc)
     cols_ref[...] = jnp.zeros_like(cols_ref)

time: 196 us -> 193 us (0.985)
  Pallas kernels: 192 us -> 184 us
  waiting for transfers between devices: 0.01 us -> 3.53 us
    pallas_call x1, Pallas kernels: 37.1 us -> 30 us  [attend_back(): pl.pallas_call(functools.partial(attend_back_kernel, size=size, blocks=ro...]
    pallas_call x1, Pallas kernels: 26.6 us -> 23 us  [attend(): pl.pallas_call(functools.partial(attend_kernel, size=size, blocks=rows //...]
    ppermute x2, waiting for transfers between devices: 0.01 us -> 3.53 us  [across(): return lax.ppermute(value, 'tp', [(n, n ^ 2) for n in range(4)])]
    pallas_call x3, Pallas kernels: 126 us -> 129 us  [comm_call(): pl.pallas_call(kernel, out_shape=out_shape, in_specs=in_specs, out_specs=...]
  transfers between devices with their start and end apart: 2 -> 2, of which waited for: 0 -> 1; matrix products, arithmetic and copies ran while one was open for 0% -> 0% of each run, Pallas kernels for 32% -> 27%
where the time goes in v3:
time: 193 us; the launch traced here: 195 us
  Pallas kernels  184 us (95%)
  local copies, waits for them, and re-layouts  4.51 us (2%)
  waiting for transfers between devices  3.53 us (2%)
    pallas_call x3, Pallas kernels, comm_call(): pl.pallas_call(kernel, out_shape=out_shape, in_specs=in_specs, out_specs=...  129 us
    pallas_call x1, Pallas kernels, attend_back(): pl.pallas_call(functools.partial(attend_back_kernel, size=size, blocks=ro...  30 us
    pallas_call x1, Pallas kernels, attend(): pl.pallas_call(functools.partial(attend_kernel, size=size, blocks=rows //...  23 us
    unnamed x9, local copies, waits for them, and re-layouts  3.88 us
  transfers between devices with their start and end apart: 2, of which 1 were waited for; matrix products, arithmetic and copies ran while one was open for 0% of the time, Pallas kernels for 27%

profile of v3, /device:TPU:0, one launch (start us, length us, event | category | flops | bytes accessed | tf_op | source)
XLA Modules:
  0.0 194.9 jit_solution(3161257545150552210)
XLA Ops:
  0.6 0.0 copy-start
  0.7 0.8 copy-done
  1.4 0.6 copy_bitcast_fusion.w0
  2.1 38.7 %enter.1 = (bf16[4096,512]{1,0:T(8,128)(2,1)}, s32[4,1,1024]{2,1,0:T(1,128)}, s32[8,128]{1,0:T(8,128)}, f32[16,512]{1,0:T(8,128)}, bf16[2,4096,128]{2,1,0:T(8,12...) custom-call(bf16[1024,512]{1,0:T(8,128)(2,1)} %x_in.1, ...), custom_call_target="tpu_custom_call" | custom-call | bytes 62914560 | tf_op jit(solution)/shard_map/enter/pallas_call | solution.py:272
  40.8 0.7 collective-permute-start
  41.5 23.0 %attend.1 = (bf16[4096,128]{1,0:T(8,128)(2,1)}, bf16[2,4096,128]{2,1,0:T(8,128)(2,1)}) custom-call(s32[8,128]{1,0:T(8,128)} %get-tuple-element.53.low_ref, bf16[2,4096,128]{2,1,0:T(8,128)(2,1)} %get-tuple-element.54.qa_ref, bf16[2,4096,128]{2,1,0:T(8,128)(2,1)} %get-tuple-element.55.ka_ref, bf16[2,80,4096]{2,1,0:T(8,128)(2,1)} %get-tuple-element.56.vt_ref, ...), custom_call_target="tpu_custom_call" | custom-call | flops 30064771072 | bytes 8388608 | tf_op jit(solution)/shard_map/attend/pallas_call | solution.py:126
  64.4 3.5 %collective-permute-done.passed_ref = bf16[512,1152]{1,0:T(8,128)(2,1)S(1)} collective-permute-done((bf16[512,1152]{1,0:T(8,128)(2,1)}, bf16[512,1152]{1,0:T(8,128)(2,1)S(1)}, u32[]{:S(2)}, u32[]{:S(2)}) %collective-permute-start) | collective-permute-done | bytes 1179680 | tf_op jit(solution)/shard_map/ppermute | solution.py:1094
  68.0 0.0 copy-start.2
  68.0 1.0 copy-done.2
  69.0 36.4 %middle.1 = (bf16[1024,512]{1,0:T(8,128)(2,1)}, f32[1024,512]{1,0:T(8,128)}, bf16[4096,128]{1,0:T(8,128)(2,1)}, bf16[512,1152]{1,0:T(8,128)(2,1)}, bf16[512,1152]{1,0:T(8,128)(2,1)}, /*index=5*/f32[8,512]{1,0:T(8,128)}) custom-call(bf16[4096,128]{1,0:T(8,128)(2,1)} %get-tuple-element.58.seq_out.o_ref, bf16[512,1152]{1,0:T(8,128)(2,1)} %bitcast.24, ...), custom_call_target="tpu_custom_call" | custom-call | bytes 62914560 | tf_op jit(solution)/shard_map/middle/pallas_call | solution.py:272
  105.4 1.1 collective-permute-start.1
  106.5 30.0 %attend_back.1.grad_ref = bf16[4096,384]{1,0:T(8,128)(2,1)} custom-call(s32[8,128]{1,0:T(8,128)} %get-tuple-element.53.low_ref, bf16[2,4096,128]{2,1,0:T(8,128)(2,1)} %get-tuple-element.62.qb_ref, bf16[2,4096,128]{2,1,0:T(8,128)(2,1)} %get-tuple-element.55.ka_ref, bf16[2,4096,128]{2,1,0:T(8,128)(2,1)} %get-tuple-element.63.va_ref, ...), custom_call_target="tpu_custom_call" | custom-call | flops 51539607552 | bytes 16777216 | tf_op jit(solution)/shard_map/attend_back/pallas_call | solution.py:217
  136.5 0.0 collective-permute-done.1
  136.5 0.0 copy-start.1
  136.5 1.1 copy-done.1
  137.6 53.7 %leave.1 = (bf16[1024,512]{1,0:T(8,128)(2,1)}, f32[64,512]{1,0:T(8,128)}, f32[64,512]{1,0:T(8,128)}, f32[64,128]{1,0:T(8,128)}, f32[64,384]{1,0:T(8,128)}, /*index=5*/f32[8,512]{1,0:T(8,128)}, f32[4,512]{1,0:T(4,128)}) custom-call(bf16[4096,384]{1,0:T(8,128)(2,1)} %attend_back.1.grad_ref, bf16[4096,512]{1,0:T(8,128)(2,1)} %get-tuple-element.66.normed_in, ...), custom_call_target="tpu_custom_call" | custom-call | bytes 62914560 | tf_op jit(solution)/shard_map/leave/pallas_call | solution.py:272
  191.3 0.0 copy-start.3
  191.3 2.6 %finish.1 = (bf16[1024,512]{1,0:T(8,128)(2,1)}, f32[64,512]{1,0:T(8,128)}, f32[64,512]{1,0:T(8,128)}, f32[64,128]{1,0:T(8,128)}, f32[3,64,128]{2,1,0:T(8,128)}, ...) custom-call(bf16[1024,512]{1,0:T(8,128)(2,1)} %get-tuple-element.72., ...), custom_call_target="tpu_custom_call" | custom-call | bytes 3145728 | tf_op jit(solution)/shard_map/finish/pallas_call | solution.py:1069
  193.9 0.0 copy-done.3
  193.9 1.0 copy.34
Async XLA Ops:
  0.6 0.8 copy-start
  40.8 27.2 %collective-permute-start = (bf16[512,1152]{1,0:T(8,128)(2,1)}, bf16[512,1152]{1,0:T(8,128)(2,1)S(1)}, u32[]{:S(2)}, u32[]{:S(2)}) collective-permute-start(bf16[512,1152]{1,0:T(8,128)(2,1)} %bitcast.23), channel_id=1, source_target_pairs={{0,2},{1,3},{2,0},{3,1},{4,6},{5,7},{6,4},{7,5},{8,10},{9,11},{10,... | collective-permute-start | bytes 3538952 | tf_op jit(solution)/shard_map/ppermute | solution.py:1094
  68.0 1.0 copy-start.2
  105.4 31.2 %collective-permute-start.1 = (bf16[512,1152]{1,0:T(8,128)(2,1)}, bf16[512,1152]{1,0:T(8,128)(2,1)S(1)}, u32[]{:S(2)}, u32[]{:S(2)}) collective-permute-start(bf16[512,1152]{1,0:T(8,128)(2,1)} %get-tuple-element.69), channel_id=1, source_target_pairs={{0,2},{1,3},{2,0},{3,1},{4,6},{5,7},{6,4},{7,5},{8,10},{9,11},{10,... | collective-permute-start | bytes 3538952 | tf_op jit(solution)/shard_map/ppermute | solution.py:1094
  136.5 1.1 copy-start.1
  191.3 2.6 %copy-start.3 = (bf16[1024,512]{1,0:T(8,128)(2,1)S(1)}, bf16[1024,512]{1,0:T(8,128)(2,1)}, u32[]{:S(2)}) copy-start(bf16[1024,512]{1,0:T(8,128)(2,1)} %get-tuple-element.106) | copy-start | bytes 3145732
